TPU v7x, 32 devices: a whole 2x2x4 slice. The times are simulated.
32 devices in a mesh: row: 8 (over z, y), col: 4 (over x, core).
Axes of the slice: x: 2, y: 2, z: 4, core: 2. Of those that a mesh axis runs over, the one named last changes fastest.
Arguments:
- basis_values: bfloat16 [128, 1024, 640], P(('row', 'col')), may hold values from -6 to 6
- potential: float32 [128, 1024], P(('row', 'col')), may hold values from -0.12 to 0.12
- block_lists: int32 [128, 5], P(('row', 'col')), may hold values from 0 to 63, as said below
- func_counts: int32 [128], P(('row', 'col')), may hold values from 576 to 640
- density_tiles: bfloat16 [8, 8, 16, 4, 128, 128], P(None, 'row', None, 'col'), may hold values from -0.0095825195 to 0.0095825195
Outputs:
- hamiltonian_tiles: float32 [8, 8, 16, 4, 128, 128], P(None, 'row', None, 'col')
- density_points: float32 [128, 1024], P(('row', 'col'))
Inputs may be any that keep to these rules, and one draw needn't show every extreme that they name: `block_lists`: each batch lists 5 different blocks whose remainders modulo 8 are 5 consecutive values (counted cyclically) starting at an even number; the 4 batches of one device start at the remainders 0, 2, ..., 6, each exactly once, in an order drawn from the seed; the quotients of the blocks by 8 are free. So in the batches of one device no owner (block row modulo 8, block column modulo 4) of a listed pair of blocks is named by more than 5 pairs, and some owner is named by exactly 5.
All inputs are finite; a program needn't handle non-finite values.
Results may differ from a plain program's by a relative error of at most 0.0029.
Values may be sent and summed in bfloat16 or wider, within the bound.
A program may use at most 320 MiB of HBM per device.

v0:
```python
import jax
import jax.numpy as jnp
from jax import lax
from jax.sharding import PartitionSpec as P


def on_device(basis_values, potential, block_lists, func_counts, density_tiles):
    rows_n = lax.axis_size("row")
    cols_n = lax.axis_size("col")
    owners = rows_n * cols_n
    per_owner = max(3, 9 - cols_n)
    slots = owners * per_owner
    nbatch, points, width = basis_values.shape
    blocks_n = block_lists.shape[1]
    block = density_tiles.shape[-1]
    nblk = density_tiles.shape[0] * rows_n
    tile_rows = density_tiles.shape[0]
    tile_cols = density_tiles.shape[2]
    tiles_n = tile_rows * tile_cols
    pairs = nbatch * blocks_n * blocks_n
    columns = jnp.arange(width, dtype=jnp.int32)
    keep = (columns[None, :] < func_counts[:, None])[:, None, :]
    masked = jnp.where(keep, basis_values, jnp.zeros_like(basis_values))
    weighted = (masked.astype(jnp.float32) * potential[:, :, None]).astype(jnp.bfloat16)
    local = jnp.einsum("bpi,bpj->bij", masked, weighted, preferred_element_type=jnp.float32)
    pieces = local.reshape(nbatch, blocks_n, block, blocks_n, block).transpose(0, 1, 3, 2, 4)
    pieces = pieces.reshape(pairs, block * block)
    first = jnp.broadcast_to(block_lists[:, :, None], (nbatch, blocks_n, blocks_n)).reshape(pairs)
    second = jnp.broadcast_to(block_lists[:, None, :], (nbatch, blocks_n, blocks_n)).reshape(pairs)
    target = first % rows_n * cols_n + second % cols_n
    onehot = (target[:, None] == jnp.arange(owners, dtype=jnp.int32)[None, :]).astype(jnp.int32)
    before = jnp.cumsum(onehot, axis=0) - onehot
    rank = jnp.sum(before * onehot, axis=1)
    slot_of = target * per_owner + rank
    source = (
        jnp.full((slots,), pairs, jnp.int32).at[slot_of].set(jnp.arange(pairs, dtype=jnp.int32))
    )
    padded = jnp.concatenate([pieces, jnp.zeros((1, block * block), jnp.float32)], axis=0)
    outgoing = padded[source]
    numbers = jnp.concatenate(
        [(first * nblk + second).astype(jnp.float32), jnp.full((1,), -1.0, jnp.float32)]
    )
    labels = numbers[source]
    arrived, arrived_labels = (
        lax.all_to_all(
            outgoing.reshape(owners, per_owner, block * block),
            ("row", "col"),
            split_axis=0,
            concat_axis=0,
            tiled=True,
        ),
        lax.all_to_all(
            labels.reshape(owners, per_owner),
            ("row", "col"),
            split_axis=0,
            concat_axis=0,
            tiled=True,
        ),
    )
    arrived = arrived.reshape(slots, block * block)
    named = arrived_labels.reshape(slots).astype(jnp.int32)
    valid = named >= 0
    safe_named = jnp.where(valid, named, 0)
    tile_index = safe_named // nblk // rows_n * tile_cols + safe_named % nblk // cols_n
    tile_index = jnp.where(valid, tile_index, -1)
    selector = (tile_index[None, :] == jnp.arange(tiles_n, dtype=jnp.int32)[:, None]).astype(
        jnp.float32
    )
    summed = jnp.dot(
        selector, arrived, precision=lax.Precision.HIGHEST, preferred_element_type=jnp.float32
    )
    hamiltonian_tiles = summed.reshape(tile_rows, 1, tile_cols, 1, block, block)
    own_tiles = density_tiles.reshape(tiles_n, block, block)
    answers = own_tiles[jnp.maximum(tile_index, 0)]
    returned = lax.all_to_all(
        answers.reshape(owners, per_owner, block, block),
        ("row", "col"),
        split_axis=0,
        concat_axis=0,
        tiled=True,
    )
    returned = returned.reshape(slots, block, block)
    fetched = returned[slot_of].reshape(nbatch, blocks_n, blocks_n, block, block)
    gathered = fetched.transpose(0, 1, 3, 2, 4).reshape(nbatch, width, width)
    product = jnp.einsum("bpi,bij->bpj", masked, gathered, preferred_element_type=jnp.float32)
    density_points = jnp.sum(product * masked.astype(jnp.float32), axis=2)
    return (hamiltonian_tiles, density_points)


def solution(mesh):
    in_specs = (
        P(("row", "col"), None, None),
        P(("row", "col"), None),
        P(("row", "col"), None),
        P(("row", "col")),
        P(None, "row", None, "col", None, None),
    )
    out_specs = (P(None, "row", None, "col", None, None), P(("row", "col"), None))
    return jax.shard_map(
        on_device, mesh=mesh, in_specs=in_specs, out_specs=out_specs, check_vma=False
    )
```

profile of v0, /device:TPU:0, one launch (start us, length us, event | category | flops | bytes accessed | tf_op | source)
XLA Modules:
  0.0 550.8 jit_solution(7486164252850688076)
XLA Ops:
  0.6 0.7 broadcast_in_dim.21
  1.4 0.1 reshape.489
  1.5 0.8 broadcast_in_dim.20
  2.6 0.1 reduce_window_sum.11
  2.7 0.2 select_reduce_fusion
  2.9 0.9 scatter_custom_fusion
  3.9 1.5 gather_fusion
  5.5 0.1 all_to_all.12
  5.6 14.3 %all_to_all.19 = f32[32,1,5]{2,1,0:T(1,128)S(1)} all-to-all(f32[32,1,5]{2,1,0:T(1,128)S(1)} %bitcast.51), channel_id=1, replica_groups=mesh['row'=8,'col'=4] {'row','col'}, dimensions={0} | all-to-all | bytes 1280 | tf_op jit(solution)/shard_map/all_to_all | solution.py:52
  19.9 0.1 convert_element_type.40
  20.1 10.0 %gather_fusion.2 = bf16[160,128,128]{2,1,0:T(8,128)(2,1)} fusion(bf16[128,128,128]{2,1,0:T(8,128)(2,1)} %bitcast.50, s32[1024]{0:T(1024)S(1)} %pad_clamp_fusion.1), kind=kCustom, calls=%fused_computation.2 | custom fusion | bytes 10486400 | tf_op jit(solution)/shard_map/gather | solution.py:74
  30.0 3.6 all-to-all-start.2
  33.6 8.0 %copy.21 = bf16[4,1024,640]{1,2,0:T(8,128)(2,1)} copy(bf16[4,1024,640]{2,1,0:T(8,128)(2,1)} %param.5) | data formatting | bytes 10485760 | tf_op args[0]
  41.7 10.3 %fusion.4 = f32[4,640,640]{2,1,0:T(8,128)} fusion(f32[4,1024]{1,0:T(4,128)S(1)} %copy-done.1, bf16[4,1024,640]{1,2,0:T(8,128)(2,1)} %copy.21, pred[4,640]{1,0:T(4,128)(4,1)S(1)} %iota_compare_fusion.1), kind=kOutput, calls=%fused_computation.12 | convolution fusion | flops 3368550400 | bytes 11815424 | tf_op jit(solution)/shard_map/bpi,bpj->bij/dot_general | solution.py:25
  51.9 8.7 %reshape.492 = f32[4,5,128,5,128]{4,3,2,1,0:T(8,128)} reshape(f32[4,640,640]{2,1,0:T(8,128)} %fusion.4) | data formatting | bytes 13107200 | tf_op jit(solution)/shard_map/reshape | solution.py:26
  60.6 5.2 copy.23
  65.8 0.9 pad.7
  66.7 4.9 copy.35
  71.6 3.4 concatenate.7
  75.0 15.0 %gather_fusion.1 = f32[160,16384]{1,0:T(8,128)} fusion(f32[101,16384]{1,0:T(8,128)} %concatenate.7, s32[1024]{0:T(1024)S(1)} %pad_clamp_fusion.2), kind=kCustom, calls=%fused_computation.1 | custom fusion | bytes 20972160 | tf_op jit(solution)/shard_map/gather | solution.py:39
  90.1 10.8 %reshape.494 = f32[32,5,16384]{2,1,0:T(8,128)} reshape(f32[160,16384]{1,0:T(8,128)} %gather_fusion.1) | data formatting | bytes 20971520 | tf_op jit(solution)/shard_map/reshape | solution.py:46
  100.8 49.3 %all-to-all-done.2 = bf16[32,5,128,128]{3,2,1,0:T(8,128)(2,1)} async-done(((bf16[32,5,128,128]{3,2,1,0:T(8,128)(2,1)}), bf16[32,5,128,128]{3,2,1,0:T(8,128)(2,1)}, u32[]{:S(2)}, u32[]{:S(2)}) %all-to-all-start.2) | async-done | bytes 5242912 | tf_op jit(solution)/shard_map/all_to_all | solution.py:75
  150.1 3.9 all-to-all-start.1
  154.1 0.1 convert_element_type.37
  154.2 3.7 gather_fusion.3
  157.9 5.2 copy.25
  163.1 7.0 %reshape.547 = bf16[4,640,640]{2,1,0:T(8,128)(2,1)S(1)} reshape(bf16[4,5,128,5,128]{4,3,2,1,0:T(8,128)(2,1)} %copy.25) | data formatting | bytes 6553600 | tf_op jit(solution)/shard_map/reshape | solution.py:84
  170.1 9.6 %fusion.1 = f32[4,1024]{1,0:T(4,128)} fusion(bf16[4,1024,640]{1,2,0:T(8,128)(2,1)} %copy.21, pred[4,640]{1,0:T(4,128)(4,1)S(1)} %iota_compare_fusion.1, bf16[4,640,640]{2,1,0:T(8,128)(2,1)S(1)} %reshape.547), kind=kOutput, calls=%fused_computation.8 | convolution fusion | flops 3368546304 | bytes 8538624 | tf_op jit(solution)/shard_map/bpi,bij->bpj/dot_general | solution.py:85
  179.6 347.0 %all-to-all-done.1 = f32[32,5,16384]{2,1,0:T(8,128)} async-done(((f32[32,5,16384]{2,1,0:T(8,128)}), f32[32,5,16384]{2,1,0:T(8,128)}, u32[]{:S(2)}, u32[]{:S(2)}) %all-to-all-start.1) | async-done | bytes 10485792 | tf_op jit(solution)/shard_map/all_to_all | solution.py:45
  526.7 10.0 %reshape.495 = f32[160,16384]{1,0:T(8,128)} reshape(f32[32,5,16384]{2,1,0:T(8,128)} %all-to-all-done.1) | data formatting | bytes 20971520 | tf_op jit(solution)/shard_map/reshape | solution.py:60
  536.6 8.3 %fusion.8 = f32[8,1,16,1,128,128]{5,2,4,0,3,1:T(8,128)S(1)} fusion(s32[8,16]{1,0:T(8,128)S(1)} %multiply_add_fusion, s32[160]{0:T(256)S(1)} %compare_select_fusion.13, f32[160,16384]{1,0:T(8,128)} %reshape.495), kind=kOutput, calls=%fused_computation.16 | convolution fusion | flops 4026552320 | bytes 18875520 | tf_op jit(solution)/shard_map/dot_general | solution.py:69
  544.9 5.9 %copy.28 = f32[8,1,16,1,128,128]{5,4,3,2,1,0:T(8,128)} copy(f32[8,1,16,1,128,128]{5,2,4,0,3,1:T(8,128)S(1)} %fusion.8) | data formatting | bytes 16777216
  (22 shorter events, 0.7 us)
Async XLA Ops:
  30.0 120.1 %all-to-all-start.2 = ((bf16[32,5,128,128]{3,2,1,0:T(8,128)(2,1)}), bf16[32,5,128,128]{3,2,1,0:T(8,128)(2,1)}, u32[]{:S(2)}, u32[]{:S(2)}) async-start(bf16[32,5,128,128]{3,2,1,0:T(8,128)(2,1)} %bitcast.48), calls=%async_computation.2 | async-start | bytes 10485760 | tf_op jit(solution)/shard_map/all_to_all | solution.py:75
  33.6 8.0 %copy-start = (s32[4]{0:T(128)S(1)}, s32[4]{0:T(128)}, u32[]{:S(2)}) copy-start(s32[4]{0:T(128)} %param.8) | copy-start | bytes 52
  33.6 8.1 %copy-start.1 = (f32[4,1024]{1,0:T(4,128)S(1)}, f32[4,1024]{1,0:T(4,128)}, u32[]{:S(2)}) copy-start(f32[4,1024]{1,0:T(4,128)} %param.6) | copy-start | bytes 49156
  150.1 376.5 %all-to-all-start.1 = ((f32[32,5,16384]{2,1,0:T(8,128)}), f32[32,5,16384]{2,1,0:T(8,128)}, u32[]{:S(2)}, u32[]{:S(2)}) async-start(f32[32,5,16384]{2,1,0:T(8,128)} %reshape.494), calls=%async_computation.1 | async-start | bytes 33554432 | tf_op jit(solution)/shard_map/all_to_all | solution.py:45
where the time goes:
time: 552 us; the launch traced here: 551 us
  waiting for transfers between devices  396 us (72%)
  local copies, waits for them, and re-layouts  103 us (19%)
  matrix products  28.1 us (5%)
  blocking collectives  14.3 us (3%)
  starting transfers between devices  7.47 us (1%)
    all_to_all x1, waiting for transfers between devices, on_device(): lax.all_to_all(outgoing.reshape(owners, per_owner, block * block), ('row'...  347 us
    all_to_all x1, waiting for transfers between devices, on_device(): lax.all_to_all(answers.reshape(owners, per_owner, block, block), ('row',...  49.3 us
    unnamed x8, local copies, waits for them, and re-layouts  19.7 us
    gather x1, local copies, waits for them, and re-layouts, on_device(): outgoing = padded[source]  15 us
    all_to_all x1, blocking collectives, on_device(): lax.all_to_all(labels.reshape(owners, per_owner), ('row', 'col'), split_a...  14.3 us
  transfers between devices with their start and end apart: 2, of which 2 were waited for; matrix products, arithmetic and copies ran while one was open for 17% of the time, Pallas kernels for 0%

commit v1 on v0

v1 whole, which is shorter than its diff:
```python
import functools

import jax
import jax.numpy as jnp
from jax import lax
from jax.experimental import pallas as pl
from jax.experimental.pallas import tpu as pltpu
from jax.sharding import PartitionSpec as P

MESH = pl.DeviceIdType.MESH
VMEM_LIMIT = 60 * 1024 * 1024


def exchange_kernel(
    rows_n,
    cols_n,
    lists_ref,
    counts_ref,
    basis_ref,
    pot_ref,
    tiles_ref,
    arrived_ref,
    lists_out,
    dens_ref,
    xs,
    ws,
    hst,
    dst,
    gathered,
    myrow,
    landed,
    alllists,
    perm_s,
    list_send,
    list_recv,
    list_local,
    h_send,
    h_recv,
    d_send,
    d_recv,
):
    nbatch, points, width = basis_ref.shape
    block = tiles_ref.shape[-1]
    nl = width // block
    ndev = rows_n * cols_n
    reps = pl.cdiv(nl, cols_n)
    heads = (nl + 1) // 2
    my_r = lax.axis_index("row")
    my_c = lax.axis_index("col")
    me = my_r * cols_n + my_c

    def dev(d):
        return {"row": d // cols_n, "col": d % cols_n}

    barrier = pltpu.get_barrier_semaphore()

    @pl.loop(1, ndev)
    def _(i):
        d = (me + i) % ndev
        pl.semaphore_signal(barrier, inc=1, device_id=dev(d), device_id_type=MESH)

    listed = [[lists_ref[b, k] for k in range(nl)] for b in range(nbatch)]
    starts, sorted_val, sorted_pos = [], [], []
    for b in range(nbatch):
        res = [v % rows_n for v in listed[b]]
        start = jnp.int32(0)
        for k in range(nl):
            pred = (res[k] + (rows_n - 1)) % rows_n
            seen = functools.reduce(
                jnp.logical_or, [pred == res[j] for j in range(nl) if j != k]
            )
            start = start + jnp.where(seen, 0, res[k])
        starts.append(start)
        offs = [(r - start + rows_n) % rows_n for r in res]
        sorted_val.append(
            [sum(jnp.where(offs[k] == o, listed[b][k], 0) for k in range(nl)) for o in range(nl)]
        )
        sorted_pos.append(
            [sum(jnp.where(offs[k] == o, k, 0) for k in range(nl)) for o in range(nl)]
        )
    lane = lax.broadcasted_iota(jnp.int32, (1, block), 1)
    row = jnp.zeros((1, block), jnp.int32)
    for t in range(nbatch):
        hit = [starts[b] == 2 * t for b in range(nbatch)]
        order = jnp.minimum(sum(jnp.where(hit[b], b, 0) for b in range(nbatch)), nbatch - 1)
        perm_s[t, nl] = order
        row = jnp.where(lane == nbatch * nl + t, order, row)
        for o in range(nl):
            perm_s[t, o] = sum(jnp.where(hit[b], sorted_pos[b][o], 0) for b in range(nbatch))
            value = sum(jnp.where(hit[b], sorted_val[b][o], 0) for b in range(nbatch))
            row = jnp.where(lane == t * nl + o, value, row)
    myrow[...] = row

    def h_compute(t):
        b = perm_s[t, nl]
        count = counts_ref[b]
        pot = pot_ref[b]
        pot_col = jnp.transpose(jnp.broadcast_to(pot, (block, points)))
        for o in range(nl):
            k = perm_s[t, o]
            xf = jnp.zeros((points, block), jnp.float32)
            for p in range(nl):
                live = jnp.logical_and(lane + p * block < count, k == p)
                xb = basis_ref[b, :, p * block : (p + 1) * block]
                xf = xf + xb.astype(jnp.float32) * jnp.where(live, 1.0, 0.0)
            xs[t, :, o * block : (o + 1) * block] = xf.astype(jnp.bfloat16)
            ws[:, o * block : (o + 1) * block] = (xf * pot_col).astype(jnp.bfloat16)
        local = lax.dot_general(
            xs[t], ws[...], (((0,), (0,)), ((), ())), preferred_element_type=jnp.float32
        )
        for k in range(nl):
            for l in range(nl):
                hst[t, k, l] = local[
                    k * block : (k + 1) * block, l * block : (l + 1) * block
                ].astype(jnp.bfloat16)

    def h_copy(t, i):
        k, l = i // nl, i % nl
        r = (2 * t + k) % rows_n
        c = (2 * t + l) % cols_n
        slot = (k // 2) * reps + l // cols_n
        return (
            r * cols_n + c,
            lambda: pltpu.make_async_remote_copy(
                src_ref=hst.at[t, k, l],
                dst_ref=arrived_ref.at[slot, me],
                send_sem=h_send,
                recv_sem=h_recv.at[slot],
                device_id={"row": r, "col": c},
                device_id_type=MESH,
            ),
            lambda: pltpu.make_async_copy(
                hst.at[t, k, l], arrived_ref.at[slot, me], h_recv.at[slot]
            ),
        )

    def h_start(t):
        @pl.loop(0, nl * nl)
        def _(i):
            d, remote, local = h_copy(t, i)

            @pl.when(d != me)
            def _():
                remote().start()

            @pl.when(d == me)
            def _():
                local().start()

    def list_copy(d):
        return pltpu.make_async_remote_copy(
            src_ref=myrow,
            dst_ref=landed.at[me],
            send_sem=list_send,
            recv_sem=list_recv,
            device_id=dev(d),
            device_id_type=MESH,
        )

    pl.semaphore_wait(barrier, ndev - 1)

    @pl.loop(1, ndev)
    def _(i):
        list_copy((me + i) % ndev).start()

    own = pltpu.make_async_copy(myrow, landed.at[me], list_recv)
    own.start()

    turn = my_r // 2 + my_c

    def t_of(i):
        return (turn + i) % nbatch

    h_compute(t_of(0))
    h_start(t_of(0))

    pltpu.make_async_copy(landed, landed, list_recv).wait()
    to_smem = pltpu.make_async_copy(landed, alllists, list_local)
    to_smem.start()
    to_smem.wait()

    def slots(action):
        for j in range(heads):
            k = 2 * j + my_r % 2
            t = (my_r // 2 - j + nbatch) % nbatch
            for q in range(reps):
                l = (my_c - 2 * t + 2 * nbatch * cols_n) % cols_n + q * cols_n

                @pl.when(jnp.logical_and(k < nl, l < nl))
                def _(j=j, q=q, k=k, l=l, t=t):
                    action(j * reps + q, t, k, l)

    @pl.loop(0, ndev)
    def _(i):
        d = (me + i) % ndev

        def stage(slot, t, k, l):
            first = alllists[d, 0, t * nl + k]
            second = alllists[d, 0, t * nl + l]
            dst[slot, d] = tiles_ref[first // rows_n, second // cols_n]

        slots(stage)

    def place(t, k, l):
        return gathered.at[
            t,
            pl.ds(pl.multiple_of(k * block, block), block),
            pl.ds(pl.multiple_of(l * block, block), block),
        ]

    def d_remote(slot, t, k, l, d):
        return pltpu.make_async_remote_copy(
            src_ref=dst.at[slot, d],
            dst_ref=place(t, k, l),
            send_sem=d_send.at[slot],
            recv_sem=d_recv.at[t],
            device_id=dev(d),
            device_id_type=MESH,
        )

    def d_local(slot, t, k, l):
        return pltpu.make_async_copy(dst.at[slot, me], place(t, k, l), d_recv.at[t])

    @pl.loop(1, ndev)
    def _(i):
        d = (me + i) % ndev
        slots(lambda slot, t, k, l: d_remote(slot, t, k, l, d).start())

    slots(lambda slot, t, k, l: d_local(slot, t, k, l).start())

    @pl.loop(1, nbatch)
    def _(i):
        h_compute(t_of(i))
        h_start(t_of(i))

    lists_out[...] = landed[...]

    chunk = min(256, points)

    @pl.loop(0, nbatch)
    def _(i):
        t = t_of(i)
        pltpu.make_async_copy(gathered.at[t], gathered.at[t], d_recv.at[t]).wait()
        for s in range(points // chunk):
            x = xs[t, s * chunk : (s + 1) * chunk, :]
            prod = jnp.dot(x, gathered[t], preferred_element_type=jnp.float32)
            prod = prod * x.astype(jnp.float32)
            part = prod[:, :block]
            for o in range(1, nl):
                part = part + prod[:, o * block : (o + 1) * block]
            dens_ref[t, :, s * chunk : (s + 1) * chunk] = jnp.sum(
                jnp.transpose(part), axis=0, keepdims=True
            )

    slots(
        lambda slot, t, k, l: pltpu.make_async_copy(
            arrived_ref.at[slot], arrived_ref.at[slot], h_recv.at[slot]
        ).wait()
    )
    slots(
        lambda slot, t, k, l: pltpu.make_async_copy(
            dst.at[slot, pl.ds(0, ndev - 1)], dst.at[slot, pl.ds(0, ndev - 1)], d_send.at[slot]
        ).wait()
    )

    @pl.loop(0, nbatch * nl * nl)
    def _(i):
        d, remote, _ = h_copy(i // (nl * nl), i % (nl * nl))

        @pl.when(d != me)
        def _():
            remote().wait_send()

    pltpu.make_async_copy(
        landed.at[pl.ds(0, ndev - 1)], landed.at[pl.ds(0, ndev - 1)], list_send
    ).wait()


def scatter_kernel(rows_n, cols_n, nbatch, nl, lists_ref, arrived_ref, dens_in, ham_ref, dens_ref):
    ndev = rows_n * cols_n
    reps = pl.cdiv(nl, cols_n)
    heads = (nl + 1) // 2
    tile_cols = ham_ref.shape[1]
    my_r = lax.axis_index("row")
    my_c = lax.axis_index("col")
    me = my_r * cols_n + my_c

    @pl.loop(0, ham_ref.shape[0])
    def _(i):
        @pl.loop(0, tile_cols)
        def _(j):
            ham_ref[i, j] = jnp.zeros(ham_ref.shape[2:], jnp.float32)

    @pl.loop(0, ndev)
    def _(d):
        for j in range(heads):
            k = 2 * j + my_r % 2
            t = (my_r // 2 - j + nbatch) % nbatch
            for q in range(reps):
                l = (my_c - 2 * t + 2 * nbatch * cols_n) % cols_n + q * cols_n

                @pl.when(jnp.logical_and(k < nl, l < nl))
                def _(j=j, q=q, k=k, l=l, t=t):
                    i0 = lists_ref[d, 0, t * nl + k] // rows_n
                    j0 = lists_ref[d, 0, t * nl + l] // cols_n
                    ham_ref[i0, j0] += arrived_ref[j * reps + q, d].astype(jnp.float32)

    for t in range(nbatch):
        b = lists_ref[me, 0, nbatch * nl + t]
        dens_ref[pl.ds(b, 1), :] = dens_in[t]


def on_device(basis_values, potential, block_lists, func_counts, density_tiles):
    rows_n = lax.axis_size("row")
    cols_n = lax.axis_size("col")
    ndev = rows_n * cols_n
    nbatch, points, width = basis_values.shape
    nl = block_lists.shape[1]
    tile_rows, _, tile_cols, _, block, _ = density_tiles.shape
    assert nbatch * 2 == rows_n and rows_n % cols_n == 0
    nslots = (nl + 1) // 2 * pl.cdiv(nl, cols_n)
    tiles = density_tiles.reshape(tile_rows, tile_cols, block, block)
    vmem = pl.BlockSpec(memory_space=pltpu.VMEM)
    smem = pl.BlockSpec(memory_space=pltpu.SMEM)
    hbm = pl.BlockSpec(memory_space=pl.ANY)
    bf16 = jnp.bfloat16
    dma = pltpu.SemaphoreType.DMA
    arrived, lists, dens = pl.pallas_call(
        functools.partial(exchange_kernel, rows_n, cols_n),
        out_shape=(
            jax.ShapeDtypeStruct((nslots, ndev, block, block), bf16),
            jax.ShapeDtypeStruct((ndev, 1, block), jnp.int32),
            jax.ShapeDtypeStruct((nbatch, 1, points), jnp.float32),
        ),
        in_specs=[smem, smem, vmem, vmem, vmem],
        out_specs=(hbm, vmem, vmem),
        scratch_shapes=[
            pltpu.VMEM((nbatch, points, width), bf16),
            pltpu.VMEM((points, width), bf16),
            pltpu.VMEM((nbatch, nl, nl, block, block), bf16),
            pltpu.VMEM((nslots, ndev, block, block), bf16),
            pltpu.VMEM((nbatch, width, width), bf16),
            pltpu.VMEM((1, block), jnp.int32),
            pltpu.VMEM((ndev, 1, block), jnp.int32),
            pltpu.SMEM((ndev, 1, block), jnp.int32),
            pltpu.SMEM((nbatch, nl + 1), jnp.int32),
            dma,
            dma,
            dma,
            dma,
            dma((nslots,)),
            dma((nslots,)),
            dma((nbatch,)),
        ],
        compiler_params=pltpu.CompilerParams(
            collective_id=0, has_side_effects=True, vmem_limit_bytes=VMEM_LIMIT
        ),
    )(block_lists, func_counts, basis_values, potential.reshape(nbatch, 1, points), tiles)
    ham, density_points = pl.pallas_call(
        functools.partial(scatter_kernel, rows_n, cols_n, nbatch, nl),
        out_shape=(
            jax.ShapeDtypeStruct((tile_rows, tile_cols, block, block), jnp.float32),
            jax.ShapeDtypeStruct((nbatch, points), jnp.float32),
        ),
        in_specs=[smem, vmem, vmem],
        out_specs=(vmem, vmem),
        compiler_params=pltpu.CompilerParams(vmem_limit_bytes=VMEM_LIMIT),
    )(lists, arrived, dens)
    return ham.reshape(tile_rows, 1, tile_cols, 1, block, block), density_points


def solution(mesh):
    in_specs = (
        P(("row", "col"), None, None),
        P(("row", "col"), None),
        P(("row", "col"), None),
        P(("row", "col")),
        P(None, "row", None, "col", None, None),
    )
    out_specs = (P(None, "row", None, "col", None, None), P(("row", "col"), None))
    return jax.shard_map(
        on_device, mesh=mesh, in_specs=in_specs, out_specs=out_specs, check_vma=False
    )
```

time: 552 us -> 186 us (0.34)
  waiting for transfers between devices: 396 us -> 0 us
  Pallas kernels: 0 us -> 182 us
  local copies, waits for them, and re-layouts: 103 us -> 1.33 us
  matrix products: 28.1 us -> 0 us
  blocking collectives: 14.3 us -> 0 us
  starting transfers between devices: 7.47 us -> 0 us
    all_to_all x2 -> x0, waiting for transfers between devices: 396 us -> none  [the longest x1 347 us: on_device(): lax.all_to_all(outgoing.reshape(owners, per_owner, block * block), ('row'...]
    pallas_call x0 -> x2, Pallas kernels: none -> 182 us  [the longest x1 170 us: on_device(): pl.pallas_call(functools.partial(exchange_kernel, rows_n, cols_n), out_sh...]
    reshape x8 -> x1, local copies, waits for them, and re-layouts: 36.7 us -> 1.33 us  [on_device(): potential.reshape(nbatch, 1, points)]
    gather x4 -> x0, local copies, waits for them, and re-layouts: 30.2 us -> none  [the longest x1 15 us: on_device(): outgoing = padded[source]]
    dot_general x3 -> x0, matrix products: 28.1 us -> none  [the longest x1 10.3 us: on_device(): jnp.einsum('bpi,bpj->bij', masked, weighted, preferred_element_type=jnp.f...]
    unnamed x8 -> x0, local copies, waits for them, and re-layouts: 19.7 us -> none
    all_to_all x1 -> x0, blocking collectives: 14.3 us -> none  [on_device(): lax.all_to_all(labels.reshape(owners, per_owner), ('row', 'col'), split_a...]
    transpose x2 -> x0, local copies, waits for them, and re-layouts: 10.3 us -> none  [the longest x1 5.18 us: on_device(): gathered = fetched.transpose(0, 1, 3, 2, 4).reshape(nbatch, width, width)]
  transfers between devices with their start and end apart: 2 -> 0, of which waited for: 2 -> 0; matrix products, arithmetic and copies ran while one was open for 17% -> 0% of each run, Pallas kernels for 0% -> 0%
where the time goes in v1:
time: 186 us; the launch traced here: 184 us
  Pallas kernels  182 us (98%)
    pallas_call x1, Pallas kernels, on_device(): pl.pallas_call(functools.partial(exchange_kernel, rows_n, cols_n), out_sh...  170 us
    pallas_call x1, Pallas kernels, on_device(): pl.pallas_call(functools.partial(scatter_kernel, rows_n, cols_n, nbatch,...  12.8 us

profile of v1, /device:TPU:0, one launch (start us, length us, event | category | flops | bytes accessed | tf_op | source)
XLA Modules:
  0.0 184.4 jit_solution(3408039184804140054)
XLA Ops:
  0.6 1.3 reshape.13.pot_ref
  2.0 169.7 %shard_map.68 = (bf16[6,32,128,128]{3,2,1,0:T(8,128)(2,1)}, s32[32,1,128]{2,1,0:T(1,128)}, f32[4,1,1024]{2,1,0:T(1,128)}) custom-call(s32[4,5]{1,0:T(4,128)} %lists_ref.1, s32[4]{0:T(128)} %counts_ref.1, bf16[4,1024,640]{2,1,0:T(8,128)(2,1)} %basis_ref.1, f32[4,1,1024]{2,1,0:T(1,128)} %reshape.13.pot_ref, bf16[8,16,128,128]{3,2,1,0:T(8,128)(2,1)} %bitcast.4), custom_call_target="tpu_custom_call" | custom-call | tf_op jit(solution)/shard_map/pallas_call | solution.py:328
  171.6 12.8 %shard_map.69 = (f32[8,16,128,128]{3,2,1,0:T(8,128)}, f32[4,1024]{1,0:T(4,128)}) custom-call(s32[32,1,128]{2,1,0:T(1,128)} %get-tuple-element.7.lists_ref, bf16[6,32,128,128]{3,2,1,0:T(8,128)(2,1)} %get-tuple-element.8.arrived_ref, f32[4,1,1024]{2,1,0:T(1,128)} %get-tuple-element.9.dens_in), custom_call_target="tpu_custom_call" | custom-call | tf_op jit(solution)/shard_map/pallas_call | solution.py:359

commit v2 on v1

--- a/solution.py
+++ b/solution.py
@@ -1,4 +1,5 @@
 import functools
+import math
 
 import jax
 import jax.numpy as jnp
@@ -115,7 +116,7 @@
                 ].astype(jnp.bfloat16)
 
     def h_copy(t, i):
-        k, l = i // nl, i % nl
+        k, l = i % nl, i // nl
         r = (2 * t + k) % rows_n
         c = (2 * t + l) % cols_n
         slot = (k // 2) * reps + l // cols_n
@@ -166,7 +167,7 @@
     own = pltpu.make_async_copy(myrow, landed.at[me], list_recv)
     own.start()
 
-    turn = my_r // 2 + my_c
+    turn = my_r // 2 + nbatch // 2
 
     def t_of(i):
         return (turn + i) % nbatch
@@ -221,9 +222,11 @@
     def d_local(slot, t, k, l):
         return pltpu.make_async_copy(dst.at[slot, me], place(t, k, l), d_recv.at[t])
 
+    stride = next(s for s in range(2 * ndev // 5, 2 * ndev) if math.gcd(s, ndev) == 1)
+
     @pl.loop(1, ndev)
     def _(i):
-        d = (me + i) % ndev
+        d = (me + i * stride) % ndev
         slots(lambda slot, t, k, l: d_remote(slot, t, k, l, d).start())
 
     slots(lambda slot, t, k, l: d_local(slot, t, k, l).start())
@@ -276,7 +279,9 @@
     ).wait()
 
 
-def scatter_kernel(rows_n, cols_n, nbatch, nl, lists_ref, arrived_ref, dens_in, ham_ref, dens_ref):
+def scatter_kernel(
+    rows_n, cols_n, nbatch, nl, lists_ref, arrived_ref, dens_in, ham_ref, dens_ref, held, sems
+):
     ndev = rows_n * cols_n
     reps = pl.cdiv(nl, cols_n)
     heads = (nl + 1) // 2
@@ -285,14 +290,7 @@
     my_c = lax.axis_index("col")
     me = my_r * cols_n + my_c
 
-    @pl.loop(0, ham_ref.shape[0])
-    def _(i):
-        @pl.loop(0, tile_cols)
-        def _(j):
-            ham_ref[i, j] = jnp.zeros(ham_ref.shape[2:], jnp.float32)
-
-    @pl.loop(0, ndev)
-    def _(d):
+    def slots(action):
         for j in range(heads):
             k = 2 * j + my_r % 2
             t = (my_r // 2 - j + nbatch) % nbatch
@@ -301,9 +299,29 @@
 
                 @pl.when(jnp.logical_and(k < nl, l < nl))
                 def _(j=j, q=q, k=k, l=l, t=t):
-                    i0 = lists_ref[d, 0, t * nl + k] // rows_n
-                    j0 = lists_ref[d, 0, t * nl + l] // cols_n
-                    ham_ref[i0, j0] += arrived_ref[j * reps + q, d].astype(jnp.float32)
+                    action(j * reps + q, t, k, l)
+
+    def load(slot):
+        return pltpu.make_async_copy(arrived_ref.at[slot], held.at[slot], sems.at[slot])
+
+    slots(lambda slot, t, k, l: load(slot).start())
+
+    @pl.loop(0, ham_ref.shape[0])
+    def _(i):
+        @pl.loop(0, tile_cols)
+        def _(j):
+            ham_ref[i, j] = jnp.zeros(ham_ref.shape[2:], jnp.float32)
+
+    def add(slot, t, k, l):
+        load(slot).wait()
+
+        @pl.loop(0, ndev)
+        def _(d):
+            i0 = lists_ref[d, 0, t * nl + k] // rows_n
+            j0 = lists_ref[d, 0, t * nl + l] // cols_n
+            ham_ref[i0, j0] += held[slot, d].astype(jnp.float32)
+
+    slots(add)
 
     for t in range(nbatch):
         b = lists_ref[me, 0, nbatch * nl + t]
@@ -362,8 +380,9 @@
             jax.ShapeDtypeStruct((tile_rows, tile_cols, block, block), jnp.float32),
             jax.ShapeDtypeStruct((nbatch, points), jnp.float32),
         ),
-        in_specs=[smem, vmem, vmem],
+        in_specs=[smem, hbm, vmem],
         out_specs=(vmem, vmem),
+        scratch_shapes=[pltpu.VMEM((nslots, ndev, block, block), bf16), dma((nslots,))],
         compiler_params=pltpu.CompilerParams(vmem_limit_bytes=VMEM_LIMIT),
     )(lists, arrived, dens)
     return ham.reshape(tile_rows, 1, tile_cols, 1, block, block), density_points

time: 186 us -> 184 us (0.989)
    pallas_call x1, Pallas kernels: 12.8 us -> 9.51 us  [on_device(): pl.pallas_call(functools.partial(scatter_kernel, rows_n, cols_n, nbatch,...]
    pallas_call x1, Pallas kernels: 170 us -> 172 us  [on_device(): pl.pallas_call(functools.partial(exchange_kernel, rows_n, cols_n), out_sh...]
where the time goes in v2:
time: 184 us; the launch traced here: 183 us
  Pallas kernels  181 us (98%)
    pallas_call x1, Pallas kernels, on_device(): pl.pallas_call(functools.partial(exchange_kernel, rows_n, cols_n), out_sh...  172 us
    pallas_call x1, Pallas kernels, on_device(): pl.pallas_call(functools.partial(scatter_kernel, rows_n, cols_n, nbatch,...  9.51 us

profile of v2, /device:TPU:0, one launch (start us, length us, event | category | flops | bytes accessed | tf_op | source)
XLA Modules:
  0.0 183.3 jit_solution(17724694382351113773)
XLA Ops:
  0.6 1.3 reshape.13.pot_ref
  2.0 171.9 %shard_map.68 = (bf16[6,32,128,128]{3,2,1,0:T(8,128)(2,1)}, s32[32,1,128]{2,1,0:T(1,128)}, f32[4,1,1024]{2,1,0:T(1,128)}) custom-call(s32[4,5]{1,0:T(4,128)} %lists_ref.1, s32[4]{0:T(128)} %counts_ref.1, bf16[4,1024,640]{2,1,0:T(8,128)(2,1)} %basis_ref.1, f32[4,1,1024]{2,1,0:T(1,128)} %reshape.13.pot_ref, bf16[8,16,128,128]{3,2,1,0:T(8,128)(2,1)} %bitcast.4), custom_call_target="tpu_custom_call" | custom-call | tf_op jit(solution)/shard_map/pallas_call | solution.py:346
  173.8 9.5 %shard_map.69 = (f32[8,16,128,128]{3,2,1,0:T(8,128)}, f32[4,1024]{1,0:T(4,128)}) custom-call(s32[32,1,128]{2,1,0:T(1,128)} %get-tuple-element.7.lists_ref, bf16[6,32,128,128]{3,2,1,0:T(8,128)(2,1)} %get-tuple-element.8.arrived_ref, f32[4,1,1024]{2,1,0:T(1,128)} %get-tuple-element.9.dens_in), custom_call_target="tpu_custom_call" | custom-call | tf_op jit(solution)/shard_map/pallas_call | solution.py:377
